TPU v7x, 32 devices: a whole 2x2x4 slice. The times are simulated.
32 devices in a mesh: section: 2 (over x), seq: 16 (over z, y, core).
Axes of the slice: x: 2, y: 2, z: 4, core: 2. Of those that a mesh axis runs over, the one named last changes fastest.
Arguments:
- prev_out: bfloat16 [2, 2048, 1792], P('section', 'seq'), may hold values from -6 to 6
- prev_grad: bfloat16 [2, 2048, 1792], P('section', 'seq'), may hold values from -6 to 6
- saved_in: bfloat16 [2, 2048, 1792], P('section', 'seq'), may hold values from -6 to 6
- seq_mix: bfloat16 [2, 128, 128], P('section'), may hold values from -0.5 to 0.5
- coeffs: float32 [2, 4, 4, 1792], P('section'), may hold values from -1 to 1
- mixer: bfloat16 [2, 1792, 448], P('section'), may hold values from -0.25 to 0.25
Outputs:
- out_fwd: bfloat16 [2, 2048, 1792], P('section', 'seq')
- out_dh: bfloat16 [2, 2048, 1792], P('section', 'seq')
- grad_w: float32 [2, 1792, 448], P('section', 'seq')
- grad_b: float32 [2, 128, 128], P('section')
All inputs are finite; a program needn't handle non-finite values.
Results may differ from a plain program's by a relative error of at most 0.01.
Values may be sent and summed in bfloat16 or wider, within the bound.
No kernel may reach another device: no remote copies, remote signals or barrier semaphores. Data moves between devices by JAX's collectives and lax.ppermute only.
A program may use at most 64 MiB of HBM per device.

v0:
```python
import jax
import jax.numpy as jnp
from jax import lax
from jax.sharding import PartitionSpec as P


def swapped(block, axis, stride):
    count = lax.axis_size(axis)
    route = []
    for low in range(count):
        high = low | 1 << stride
        if high != low and high < count:
            route += [(low, high), (high, low)]
    return lax.ppermute(block, axis, route)


def from_behind(block, axis, distance):
    devices = range(lax.axis_size(axis))
    route = [((i - distance) % len(devices), i) for i in devices]
    return lax.ppermute(block, axis, route)


def mix_forward(state, factors):
    position = lax.axis_index("seq")
    number = lax.axis_size("seq").bit_length() - 1
    for bit_level in range(number):
        partner = swapped(state, "seq", bit_level)
        upper_side = jnp.bitwise_and(jnp.right_shift(position, bit_level), 1) == 1
        own_vals = state.astype(jnp.float32)
        partner_vals = partner.astype(jnp.float32)
        as_lower = factors[bit_level, 0] * own_vals + factors[bit_level, 1] * partner_vals
        as_upper = factors[bit_level, 2] * partner_vals + factors[bit_level, 3] * own_vals
        state = jnp.where(upper_side, as_upper, as_lower).astype(jnp.bfloat16)
    return state


def mix_adjoint(state, factors):
    position = lax.axis_index("seq")
    number = lax.axis_size("seq").bit_length() - 1
    for bit_level in reversed(range(number)):
        partner = swapped(state, "seq", bit_level)
        upper_side = jnp.bitwise_and(jnp.right_shift(position, bit_level), 1) == 1
        own_vals = state.astype(jnp.float32)
        partner_vals = partner.astype(jnp.float32)
        as_lower = factors[bit_level, 0] * own_vals + factors[bit_level, 2] * partner_vals
        as_upper = factors[bit_level, 1] * partner_vals + factors[bit_level, 3] * own_vals
        state = jnp.where(upper_side, as_upper, as_lower).astype(jnp.bfloat16)
    return state


def block_apply(rows, blocks):
    block_len = blocks.shape[0]
    shaped = rows.reshape(-1, block_len, rows.shape[1])
    mixed = jnp.einsum("ij,bjd->bid", blocks, shaped, preferred_element_type=jnp.float32)
    return mixed.reshape(rows.shape).astype(jnp.bfloat16)


def layer_forward(rows, blocks, factors, weights):
    width = rows.shape[1]
    block_width = weights.shape[1]
    nblocks = width // block_width
    blocked = block_apply(rows, blocks)
    state = mix_forward(blocked, factors)
    act = (rows.astype(jnp.float32) + state.astype(jnp.float32)).astype(jnp.bfloat16)
    act3 = act.reshape(-1, nblocks, block_width)
    weight3 = weights.reshape(nblocks, block_width, block_width)
    pre = jnp.einsum("tbi,bio->tbo", act3, weight3, preferred_element_type=jnp.float32)
    return (act3, pre)


def on_device(prev_out, prev_grad, saved_in, seq_mix, coeffs, mixer):
    incoming = from_behind(prev_out, "section", 1)[0]
    upstream = from_behind(prev_grad, "section", -1)[0]
    blocks = seq_mix[0]
    factors = coeffs[0]
    weights = mixer[0]
    rows_dev, width = incoming.shape
    block_width = weights.shape[1]
    nblocks = width // block_width
    block_len = blocks.shape[0]
    act3, pre = layer_forward(incoming, blocks, factors, weights)
    result = (
        (act3.astype(jnp.float32) + jax.nn.silu(pre)).reshape(rows_dev, width).astype(jnp.bfloat16)
    )
    stored = saved_in[0]
    act_two, pre_two = layer_forward(stored, blocks, factors, weights)
    sigma = jax.nn.sigmoid(pre_two)
    gz = (
        upstream.astype(jnp.float32).reshape(-1, nblocks, block_width)
        * (sigma * (1.0 + pre_two * (1.0 - sigma)))
    ).astype(jnp.bfloat16)
    weight3 = weights.reshape(nblocks, block_width, block_width)
    back = jnp.einsum("tbo,bio->tbi", gz, weight3, preferred_element_type=jnp.float32)
    d_act = (upstream.astype(jnp.float32) + back.reshape(rows_dev, width)).astype(jnp.bfloat16)
    weight_term = jnp.einsum(
        "tbi,tbo->bio", act_two, gz, preferred_element_type=jnp.float32
    ).reshape(width, block_width)
    grad_weight = lax.psum_scatter(weight_term, "seq", scatter_dimension=0, tiled=True)
    dblocked = mix_adjoint(d_act, factors)
    dblk = dblocked.reshape(-1, block_len, width)
    stored_blk = stored.reshape(-1, block_len, width)
    block_term = jnp.einsum("bid,bjd->ij", dblk, stored_blk, preferred_element_type=jnp.float32)
    grad_block = lax.psum(block_term, "seq")
    through = jnp.einsum("ij,bid->bjd", blocks, dblk, preferred_element_type=jnp.float32).reshape(
        rows_dev, width
    )
    in_grad = (d_act.astype(jnp.float32) + through).astype(jnp.bfloat16)
    return (result[None], in_grad[None], grad_weight[None], grad_block[None])


def solution(mesh):
    placed = (
        P("section", "seq", None),
        P("section", "seq", None),
        P("section", "seq", None),
        P("section", None, None),
        P("section", None, None, None),
        P("section", None, None),
    )
    return jax.shard_map(
        on_device,
        mesh=mesh,
        in_specs=placed,
        out_specs=(
            P("section", "seq", None),
            P("section", "seq", None),
            P("section", "seq", None),
            P("section", None, None),
        ),
        check_vma=False,
    )
```

profile of v0, /device:TPU:0, one launch (start us, length us, event | category | flops | bytes accessed | tf_op | source)
XLA Modules:
  0.0 301.7 jit_solution(15228928650524788524)
XLA Ops:
  7.2 0.0 all-reduce.2.cloned.1.call-start
  7.2 0.7 copy-done
  7.9 1.3 fusion.1
  9.3 0.5 collective-permute-start.6
  9.8 1.3 slice_reduce_fusion.15
  11.1 0.1 collective-permute-done.6
  11.2 1.3 fusion.20
  12.6 3.0 collective-permute-start.7
  15.5 10.8 %collective-permute-done.7 = bf16[128,1792]{0,1:T(8,128)(2,1)S(1)} collective-permute-done((bf16[128,1792]{0,1:T(8,128)(2,1)S(1)}, bf16[128,1792]{0,1:T(8,128)(2,1)S(1)}, u32[]{:S(2)}, u32[]{:S(2)}) %collective-permute-start.7) | collective-permute-done | bytes 458784 | tf_op jit(solution)/shard_map/ppermute | solution.py:14
  26.4 1.3 fusion.24
  27.7 1.9 collective-permute-start.8
  29.6 10.3 %collective-permute-done.8 = bf16[128,1792]{0,1:T(8,128)(2,1)S(1)} collective-permute-done((bf16[128,1792]{0,1:T(8,128)(2,1)S(1)}, bf16[128,1792]{0,1:T(8,128)(2,1)S(1)}, u32[]{:S(2)}, u32[]{:S(2)}) %collective-permute-start.8) | collective-permute-done | bytes 458784 | tf_op jit(solution)/shard_map/ppermute | solution.py:14
  39.8 1.3 fusion.28
  41.2 2.6 collective-permute-start.9
  43.7 1.0 copy.12
  44.7 1.5 collective-permute-start.5
  46.2 1.0 copy.13
  47.2 2.8 copy.18
  50.0 13.3 %collective-permute-done.9 = bf16[128,1792]{0,1:T(8,128)(2,1)} collective-permute-done((bf16[128,1792]{0,1:T(8,128)(2,1)S(1)}, bf16[128,1792]{0,1:T(8,128)(2,1)}, u32[]{:S(2)}, u32[]{:S(2)}) %collective-permute-start.9) | collective-permute-done | bytes 458784 | tf_op jit(solution)/shard_map/ppermute | solution.py:14
  63.2 3.0 add_convert_fusion.1
  66.2 0.8 convolution_bitcast_fusion.1
  67.1 0.7 fusion.59
  67.8 0.2 copy-done.6
  68.0 0.9 copy-done.4
  68.9 0.1 fusion.50
  69.0 0.1 collective-permute-start.10
  69.1 22.5 %collective-permute-done.10 = bf16[128,1792]{0,1:T(8,128)(2,1)S(1)} collective-permute-done((bf16[128,1792]{0,1:T(8,128)(2,1)S(1)}, bf16[128,1792]{0,1:T(8,128)(2,1)S(1)}, u32[]{:S(2)}, u32[]{:S(2)}) %collective-permute-start.10) | collective-permute-done | bytes 458784 | tf_op jit(solution)/shard_map/ppermute | solution.py:14
  91.6 2.2 fusion.36
  93.8 2.0 copy.10
  95.8 0.6 collective-permute-start
  96.4 9.0 %collective-permute-done.11 = bf16[128,1792]{0,1:T(8,128)(2,1)} collective-permute-done((bf16[128,1792]{0,1:T(8,128)(2,1)}, bf16[128,1792]{0,1:T(8,128)(2,1)}, u32[]{:S(2)}, u32[]{:S(2)}) %collective-permute-start.11) | collective-permute-done | bytes 458784 | tf_op jit(solution)/shard_map/ppermute | solution.py:14
  105.5 2.9 fusion.40
  108.3 0.1 collective-permute-start.12
  108.4 0.3 fusion
  108.7 0.1 collective-permute-start.1
  108.8 10.0 %collective-permute-done.12 = bf16[128,1792]{0,1:T(8,128)(2,1)S(1)} collective-permute-done((bf16[128,1792]{0,1:T(8,128)(2,1)S(1)}, bf16[128,1792]{0,1:T(8,128)(2,1)S(1)}, u32[]{:S(2)}, u32[]{:S(2)}) %collective-permute-start.12) | collective-permute-done | bytes 458784 | tf_op jit(solution)/shard_map/ppermute | solution.py:14
  118.8 1.3 fusion.44
  120.2 0.1 collective-permute-start.13
  120.3 1.8 collective-permute-done.13
  122.0 2.2 fusion.48
  124.3 0.8 copy-done.2
  125.0 1.0 convolution_bitcast_fusion.3
  126.0 0.0 all-reduce.2.cloned.1.call-update
  126.0 0.2 reduce-scatter.2.cloned.1.call-start
  126.3 3.7 %fusion.58 = f32[4,448,448]{2,1,0:T(8,128)} fusion(bf16[128,4,448]{0,2,1:T(8,128)(2,1)S(1)} %bitcast.83, f32[128,4,448]{0,2,1:T(8,128)} %copy-done.6, bf16[128,4,448]{0,2,1:T(8,128)(2,1)S(1)} %bitcast.81), kind=kOutput, calls=%fused_computation.135 | convolution fusion | flops 207814656 | bytes 5046272 | tf_op jit(solution)/shard_map/tbi,tbo->bio/dot_general | solution.py:95
  129.9 0.0 reduce-scatter.2.cloned.1.call-update
  130.0 1.0 copy-done.9
  131.0 0.3 collective-permute-start.2
  131.3 12.5 %collective-permute-done.2 = bf16[128,1792]{0,1:T(8,128)(2,1)S(1)} collective-permute-done((bf16[128,1792]{0,1:T(8,128)(2,1)S(1)}, bf16[128,1792]{0,1:T(8,128)(2,1)S(1)}, u32[]{:S(2)}, u32[]{:S(2)}) %collective-permute-start.2) | collective-permute-done | bytes 458784 | tf_op jit(solution)/shard_map/ppermute | solution.py:14
  143.7 1.3 fusion.8
  145.1 0.6 collective-permute-start.3
  145.7 0.3 convolution_bitcast_fusion
  146.0 11.1 %collective-permute-done.3 = bf16[128,1792]{0,1:T(8,128)(2,1)S(1)} collective-permute-done((bf16[128,1792]{0,1:T(8,128)(2,1)S(1)}, bf16[128,1792]{0,1:T(8,128)(2,1)S(1)}, u32[]{:S(2)}, u32[]{:S(2)}) %collective-permute-start.3) | collective-permute-done | bytes 458784 | tf_op jit(solution)/shard_map/ppermute | solution.py:14
  157.1 2.2 fusion.12
  159.3 2.6 collective-permute-start.4
  161.9 0.2 add_convert_fusion
  162.1 1.0 copy.17
  163.1 18.6 %collective-permute-done.4 = bf16[128,1792]{0,1:T(8,128)(2,1)} collective-permute-done((bf16[128,1792]{0,1:T(8,128)(2,1)}, bf16[128,1792]{0,1:T(8,128)(2,1)}, u32[]{:S(2)}, u32[]{:S(2)}) %collective-permute-start.4) | collective-permute-done | bytes 458784 | tf_op jit(solution)/shard_map/ppermute | solution.py:14
  181.7 2.9 add_convert_fusion.3
  184.5 0.9 add_convert_fusion.2
  185.4 1.0 copy.16
  186.4 31.9 %all-reduce.2.cloned.1.call-done = f32[1,128,128]{2,1,0:T(8,128)} async-done(((f32[1,128,128]{2,1,0:T(8,128)}), f32[1,128,128]{2,1,0:T(8,128)}) %all-reduce.2.cloned.1.call-update) | async-done | bytes 65552 | tf_op jit(solution)/shard_map/psum | solution.py:103
  218.3 75.1 %reduce-scatter.2.cloned.1.call-done = f32[112,448]{1,0:T(8,128)} async-done(((f32[1792,448]{1,0:T(8,128)}), f32[112,448]{1,0:T(8,128)}) %reduce-scatter.2.cloned.1.call-update) | async-done | bytes 200720 | tf_op jit(solution)/shard_map/reduce_scatter | solution.py:98
  293.4 1.5 copy.20
  (23 shorter events, 0.1 us)
Async XLA Ops:
  7.2 0.8 copy-start
  7.2 211.1 %all-reduce.2.cloned.1.call-start = ((), (), s32[]{:S(2)}) async-start(), calls=%async_computation.2 | async-start | bytes 131072 | tf_op jit(solution)/shard_map/psum | solution.py:103
  9.3 2.0 collective-permute-start.6
  11.2 32.5 %copy-start.11 = (bf16[1,128,1792]{2,1,0:T(8,128)(2,1)S(1)}, bf16[1,128,1792]{2,1,0:T(8,128)(2,1)}, u32[]{:S(2)}) copy-start(bf16[1,128,1792]{2,1,0:T(8,128)(2,1)} %param.7) | copy-start | bytes 1376260
  12.6 13.8 %collective-permute-start.7 = (bf16[128,1792]{0,1:T(8,128)(2,1)S(1)}, bf16[128,1792]{0,1:T(8,128)(2,1)S(1)}, u32[]{:S(2)}, u32[]{:S(2)}) collective-permute-start(bf16[128,1792]{0,1:T(8,128)(2,1)S(1)} %fusion.20), channel_id=1, source_target_pairs={{0,2},{2,0},{1,3},{3,1},{4,6},{6,4},{5,7},{7,5},{8,10},{10,8},{9,1... | collective-permute-start | bytes 1376264 | tf_op jit(solution)/shard_map/ppermute | solution.py:14
  26.3 19.9 %copy-start.1 = (bf16[1,128,1792]{2,1,0:T(8,128)(2,1)S(1)}, bf16[1,128,1792]{2,1,0:T(8,128)(2,1)}, u32[]{:S(2)}) copy-start(bf16[1,128,1792]{2,1,0:T(8,128)(2,1)} %param.8) | copy-start | bytes 1376260
  27.7 12.1 %collective-permute-start.8 = (bf16[128,1792]{0,1:T(8,128)(2,1)S(1)}, bf16[128,1792]{0,1:T(8,128)(2,1)S(1)}, u32[]{:S(2)}, u32[]{:S(2)}) collective-permute-start(bf16[128,1792]{0,1:T(8,128)(2,1)S(1)} %fusion.24), channel_id=1, source_target_pairs={{0,4},{4,0},{1,5},{5,1},{2,6},{6,2},{3,7},{7,3},{8,12},{12,8},{9,1... | collective-permute-start | bytes 1376264 | tf_op jit(solution)/shard_map/ppermute | solution.py:14
  41.2 8.8 %copy-start.10 = (bf16[128,1792]{0,1:T(8,128)(2,1)}, bf16[128,1792]{0,1:T(8,128)(2,1)S(1)}, u32[]{:S(2)}) copy-start(bf16[128,1792]{0,1:T(8,128)(2,1)S(1)} %fusion.28) | copy-start | bytes 1376260
  41.2 22.1 %collective-permute-start.9 = (bf16[128,1792]{0,1:T(8,128)(2,1)S(1)}, bf16[128,1792]{0,1:T(8,128)(2,1)}, u32[]{:S(2)}, u32[]{:S(2)}) collective-permute-start(bf16[128,1792]{0,1:T(8,128)(2,1)S(1)} %fusion.28), channel_id=1, source_target_pairs={{0,8},{8,0},{1,9},{9,1},{2,10},{10,2},{3,11},{11,3},{4,12},{12,4},... | collective-permute-start | bytes 1376264 | tf_op jit(solution)/shard_map/ppermute | solution.py:14
  44.7 22.4 %collective-permute-start.5 = (bf16[1,128,1792]{1,2,0:T(8,128)(2,1)}, bf16[1,128,1792]{1,2,0:T(8,128)(2,1)S(1)}, u32[]{:S(2)}, u32[]{:S(2)}) collective-permute-start(bf16[1,128,1792]{1,2,0:T(8,128)(2,1)} %copy.12), channel_id=1, source_target_pairs={{16,0},{0,16},{17,1},{1,17},{18,2},{2,18},{19,3},{3,19},{20,4},{4,... | collective-permute-start | bytes 1376264 | tf_op jit(solution)/shard_map/ppermute | solution.py:20
  67.1 0.9 copy-start.6
  68.0 0.9 copy-start.4
  69.0 22.6 %collective-permute-start.10 = (bf16[128,1792]{0,1:T(8,128)(2,1)S(1)}, bf16[128,1792]{0,1:T(8,128)(2,1)S(1)}, u32[]{:S(2)}, u32[]{:S(2)}) collective-permute-start(bf16[128,1792]{0,1:T(8,128)(2,1)S(1)} %fusion.50), channel_id=1, source_target_pairs={{0,8},{8,0},{1,9},{9,1},{2,10},{10,2},{3,11},{11,3},{4,12},{12,4},... | collective-permute-start | bytes 1376264 | tf_op jit(solution)/shard_map/ppermute | solution.py:14
  93.8 11.6 %collective-permute-start.11 = (bf16[128,1792]{0,1:T(8,128)(2,1)}, bf16[128,1792]{0,1:T(8,128)(2,1)}, u32[]{:S(2)}, u32[]{:S(2)}) collective-permute-start(bf16[128,1792]{0,1:T(8,128)(2,1)} %fusion.36), channel_id=1, source_target_pairs={{0,4},{4,0},{1,5},{5,1},{2,6},{6,2},{3,7},{7,3},{8,12},{12,8},{9,1... | collective-permute-start | bytes 1376264 | tf_op jit(solution)/shard_map/ppermute | solution.py:14
  95.8 12.6 %collective-permute-start = (bf16[1,128,1792]{1,2,0:T(8,128)(2,1)}, bf16[1,128,1792]{1,2,0:T(8,128)(2,1)S(1)}, u32[]{:S(2)}, u32[]{:S(2)}) collective-permute-start(bf16[1,128,1792]{1,2,0:T(8,128)(2,1)} %copy.10), channel_id=1, source_target_pairs={{16,0},{0,16},{17,1},{1,17},{18,2},{2,18},{19,3},{3,19},{20,4},{4,... | collective-permute-start | bytes 1376264 | tf_op jit(solution)/shard_map/ppermute | solution.py:20
  108.3 10.5 %collective-permute-start.12 = (bf16[128,1792]{0,1:T(8,128)(2,1)S(1)}, bf16[128,1792]{0,1:T(8,128)(2,1)S(1)}, u32[]{:S(2)}, u32[]{:S(2)}) collective-permute-start(bf16[128,1792]{0,1:T(8,128)(2,1)S(1)} %fusion.40), channel_id=1, source_target_pairs={{0,2},{2,0},{1,3},{3,1},{4,6},{6,4},{5,7},{7,5},{8,10},{10,8},{9,1... | collective-permute-start | bytes 1376264 | tf_op jit(solution)/shard_map/ppermute | solution.py:14
  108.4 11.8 %copy-start.7 = (bf16[1,128,1792]{1,2,0:T(8,128)(2,1)}, bf16[1,128,1792]{1,2,0:T(8,128)(2,1)S(1)}, u32[]{:S(2)}) copy-start(bf16[1,128,1792]{1,2,0:T(8,128)(2,1)S(1)} %collective-permute-done) | copy-start | bytes 1376260
  108.7 11.5 %collective-permute-start.1 = (bf16[128,1792]{0,1:T(8,128)(2,1)S(1)}, bf16[128,1792]{0,1:T(8,128)(2,1)S(1)}, u32[]{:S(2)}, u32[]{:S(2)}) collective-permute-start(bf16[128,1792]{0,1:T(8,128)(2,1)S(1)} %fusion), channel_id=1, source_target_pairs={{0,1},{1,0},{2,3},{3,2},{4,5},{5,4},{6,7},{7,6},{8,9},{9,8},{10,11... | collective-permute-start | bytes 1376264 | tf_op jit(solution)/shard_map/ppermute | solution.py:14
  120.2 1.9 collective-permute-start.13
  124.3 0.8 copy-start.2
  126.0 167.3 %reduce-scatter.2.cloned.1.call-start = ((), (), s32[]{:S(2)}) async-start(), calls=%async_computation.1 | async-start | bytes 3899392 | tf_op jit(solution)/shard_map/reduce_scatter | solution.py:98
  129.9 1.0 copy-start.9
  129.9 15.8 %copy-start.3 = (bf16[128,1792]{0,1:T(8,128)(2,1)S(1)}, bf16[128,1792]{0,1:T(8,128)(2,1)}, u32[]{:S(2)}) copy-start(bf16[128,1792]{0,1:T(8,128)(2,1)} %copy-done.2) | copy-start | bytes 1376260
  131.0 31.0 %copy-start.5 = (f32[4,128,448]{1,2,0:T(8,128)S(1)}, f32[4,128,448]{1,2,0:T(8,128)}, u32[]{:S(2)}) copy-start(f32[4,128,448]{1,2,0:T(8,128)} %copy-done.4) | copy-start | bytes 2752516
  131.0 12.8 %collective-permute-start.2 = (bf16[128,1792]{0,1:T(8,128)(2,1)S(1)}, bf16[128,1792]{0,1:T(8,128)(2,1)S(1)}, u32[]{:S(2)}, u32[]{:S(2)}) collective-permute-start(bf16[128,1792]{0,1:T(8,128)(2,1)S(1)} %copy-done.9), channel_id=1, source_target_pairs={{0,2},{2,0},{1,3},{3,1},{4,6},{6,4},{5,7},{7,5},{8,10},{10,8},{9,1... | collective-permute-start | bytes 1376264 | tf_op jit(solution)/shard_map/ppermute | solution.py:14
  145.1 12.0 %collective-permute-start.3 = (bf16[128,1792]{0,1:T(8,128)(2,1)S(1)}, bf16[128,1792]{0,1:T(8,128)(2,1)S(1)}, u32[]{:S(2)}, u32[]{:S(2)}) collective-permute-start(bf16[128,1792]{0,1:T(8,128)(2,1)S(1)} %fusion.8), channel_id=1, source_target_pairs={{0,4},{4,0},{1,5},{5,1},{2,6},{6,2},{3,7},{7,3},{8,12},{12,8},{9,1... | collective-permute-start | bytes 1376264 | tf_op jit(solution)/shard_map/ppermute | solution.py:14
  159.3 22.3 %collective-permute-start.4 = (bf16[128,1792]{0,1:T(8,128)(2,1)}, bf16[128,1792]{0,1:T(8,128)(2,1)}, u32[]{:S(2)}, u32[]{:S(2)}) collective-permute-start(bf16[128,1792]{0,1:T(8,128)(2,1)} %fusion.12), channel_id=1, source_target_pairs={{0,8},{8,0},{1,9},{9,1},{2,10},{10,2},{3,11},{11,3},{4,12},{12,4},... | collective-permute-start | bytes 1376264 | tf_op jit(solution)/shard_map/ppermute | solution.py:14
  161.9 19.7 %copy-start.8 = (bf16[1,128,1792]{1,2,0:T(8,128)(2,1)S(1)}, bf16[1,128,1792]{1,2,0:T(8,128)(2,1)}, u32[]{:S(2)}) copy-start(bf16[1,128,1792]{1,2,0:T(8,128)(2,1)} %copy-done.7) | copy-start | bytes 1376260
Sparse Core Ops, SparseCore 0:
  126.2 92.0 all-reduce.1
  223.2 70.1 reduce-scatter.1
where the time goes:
time: 302 us
  waiting for transfers between devices  227 us (75%)
  other arithmetic  22.3 us (7%)
  local copies, waits for them, and re-layouts  15.1 us (5%)
  between operations  14.3 us (5%)
  starting transfers between devices  14.1 us (5%)
  matrix products  8.92 us (3%)
    ppermute x12, waiting for transfers between devices, swapped(): return lax.ppermute(block, axis, route)  120 us
    reduce_scatter x1, waiting for transfers between devices, on_device(): lax.psum_scatter(weight_term, 'seq', scatter_dimension=0, tiled=True)  75.1 us
    psum x1, waiting for transfers between devices, on_device(): grad_block = lax.psum(block_term, 'seq')  31.9 us
    ppermute x12, starting transfers between devices, swapped(): return lax.ppermute(block, axis, route)  11.7 us
    unnamed x30, local copies, waits for them, and re-layouts  11 us
    convert_element_type x4, other arithmetic, mix_adjoint(): state = jnp.where(upper_side, as_upper, as_lower).astype(jnp.bfloat16)  8.65 us
    convert_element_type x5, other arithmetic, mix_forward(): state = jnp.where(upper_side, as_upper, as_lower).astype(jnp.bfloat16)  7.57 us
  transfers between devices with their start and end apart: 16, of which 13 were waited for; matrix products, arithmetic and copies ran while one was open for 10% of the time, Pallas kernels for 0%

commit v1 on v0

--- a/solution.py
+++ b/solution.py
@@ -1,7 +1,20 @@
+import functools
 import jax
 import jax.numpy as jnp
 from jax import lax
 from jax.sharding import PartitionSpec as P
+
+
+def direct_state_on(point, dev_axis):
+    nd = lax.axis_size(dev_axis)
+    block_last = point
+    for j in [[(ix, ix ^ i0) for ix in range(nd)] for i0 in (1, 2, 4, 8, 16) if i0 < nd]:
+        arr_out = lax.ppermute(block_last, axis_name=dev_axis, perm=j)
+        block_last = block_last + arr_out
+    return block_last
+
+
+reach_trees_now = functools.partial(direct_state_on, dev_axis="seq")
 
 
 def swapped(block, axis, stride):
@@ -100,7 +113,7 @@
     dblk = dblocked.reshape(-1, block_len, width)
     stored_blk = stored.reshape(-1, block_len, width)
     block_term = jnp.einsum("bid,bjd->ij", dblk, stored_blk, preferred_element_type=jnp.float32)
-    grad_block = lax.psum(block_term, "seq")
+    grad_block = reach_trees_now(block_term)
     through = jnp.einsum("ij,bid->bjd", blocks, dblk, preferred_element_type=jnp.float32).reshape(
         rows_dev, width
     )

time: 302 us -> 216 us (0.72)
  waiting for transfers between devices: 227 us -> 139 us
  other arithmetic: 22.3 us -> 25.9 us
    reduce_scatter x1, waiting for transfers between devices: 75.1 us -> 0.01 us  [on_device(): lax.psum_scatter(weight_term, 'seq', scatter_dimension=0, tiled=True)]
    psum x1 -> x0, waiting for transfers between devices: 31.9 us -> none  [on_device(): grad_block = lax.psum(block_term, 'seq')]
    ppermute x0 -> x4, waiting for transfers between devices: none -> 24.8 us  [direct_state_on(): arr_out = lax.ppermute(block_last, axis_name=dev_axis, perm=j)]
    ppermute x12, waiting for transfers between devices: 120 us -> 114 us  [swapped(): return lax.ppermute(block, axis, route)]
    ppermute x0 -> x4, starting transfers between devices: none -> 3.37 us  [direct_state_on(): arr_out = lax.ppermute(block_last, axis_name=dev_axis, perm=j)]
    unnamed x30 -> x25, local copies, waits for them, and re-layouts: 11 us -> 8.51 us
  transfers between devices with their start and end apart: 16 -> 19, of which waited for: 13 -> 13; matrix products, arithmetic and copies ran while one was open for 10% -> 16% of each run, Pallas kernels for 0% -> 0%
where the time goes in v1:
time: 216 us; the launch traced here: 215 us
  waiting for transfers between devices  139 us (64%)
  other arithmetic  25.9 us (12%)
  starting transfers between devices  16.1 us (7%)
  between operations  14.3 us (7%)
  local copies, waits for them, and re-layouts  12.6 us (6%)
  matrix products  7.88 us (4%)
    ppermute x12, waiting for transfers between devices, swapped(): return lax.ppermute(block, axis, route)  114 us
    ppermute x4, waiting for transfers between devices, direct_state_on(): arr_out = lax.ppermute(block_last, axis_name=dev_axis, perm=j)  24.8 us
    convert_element_type x4, other arithmetic, mix_adjoint(): state = jnp.where(upper_side, as_upper, as_lower).astype(jnp.bfloat16)  11.6 us
    ppermute x12, starting transfers between devices, swapped(): return lax.ppermute(block, axis, route)  10.6 us
    unnamed x25, local copies, waits for them, and re-layouts  8.51 us
    convert_element_type x5, other arithmetic, mix_forward(): state = jnp.where(upper_side, as_upper, as_lower).astype(jnp.bfloat16)  7.57 us
    convert_element_type x2, other arithmetic, layer_forward(): (rows.astype(jnp.float32) + state.astype(jnp.float32)).astype(jnp.bfloat16)  5.86 us
  transfers between devices with their start and end apart: 19, of which 13 were waited for; matrix products, arithmetic and copies ran while one was open for 16% of the time, Pallas kernels for 0%

profile of v1, /device:TPU:0, one launch (start us, length us, event | category | flops | bytes accessed | tf_op | source)
XLA Modules:
  0.0 215.3 jit_solution(17736264543012038501)
XLA Ops:
  7.2 0.0 copy-start
  7.2 0.0 reduce-scatter.2.cloned.1.call-start
  7.2 0.7 copy-done
  7.9 1.3 fusion.1
  9.3 0.5 collective-permute-start.6
  9.8 1.3 slice_reduce_fusion.15
  11.1 0.1 collective-permute-done.6
  11.2 1.3 fusion.20
  12.6 3.0 %collective-permute-start.7 = (bf16[128,1792]{0,1:T(8,128)(2,1)S(1)}, bf16[128,1792]{0,1:T(8,128)(2,1)S(1)}, u32[]{:S(2)}, u32[]{:S(2)}) collective-permute-start(bf16[128,1792]{0,1:T(8,128)(2,1)S(1)} %fusion.20), channel_id=1, source_target_pairs={{0,2},{2,0},{1,3},{3,1},{4,6},{6,4},{5,7},{7,5},{8,10},{10,8},{9,1... | collective-permute-start | bytes 1376264 | tf_op jit(solution)/shard_map/ppermute | solution.py:27
  15.5 10.8 %collective-permute-done.7 = bf16[128,1792]{0,1:T(8,128)(2,1)S(1)} collective-permute-done((bf16[128,1792]{0,1:T(8,128)(2,1)S(1)}, bf16[128,1792]{0,1:T(8,128)(2,1)S(1)}, u32[]{:S(2)}, u32[]{:S(2)}) %collective-permute-start.7) | collective-permute-done | bytes 458784 | tf_op jit(solution)/shard_map/ppermute | solution.py:27
  26.3 1.3 fusion.24
  27.7 1.9 collective-permute-start.8
  29.6 10.3 %collective-permute-done.8 = bf16[128,1792]{0,1:T(8,128)(2,1)S(1)} collective-permute-done((bf16[128,1792]{0,1:T(8,128)(2,1)S(1)}, bf16[128,1792]{0,1:T(8,128)(2,1)S(1)}, u32[]{:S(2)}, u32[]{:S(2)}) %collective-permute-start.8) | collective-permute-done | bytes 458784 | tf_op jit(solution)/shard_map/ppermute | solution.py:27
  39.8 1.3 fusion.28
  41.2 2.6 %collective-permute-start.9 = (bf16[128,1792]{0,1:T(8,128)(2,1)S(1)}, bf16[128,1792]{0,1:T(8,128)(2,1)}, u32[]{:S(2)}, u32[]{:S(2)}) collective-permute-start(bf16[128,1792]{0,1:T(8,128)(2,1)S(1)} %fusion.28), channel_id=1, source_target_pairs={{0,8},{8,0},{1,9},{9,1},{2,10},{10,2},{3,11},{11,3},{4,12},{12,4},... | collective-permute-start | bytes 1376264 | tf_op jit(solution)/shard_map/ppermute | solution.py:27
  43.7 1.0 copy.12
  44.7 1.5 collective-permute-start.5
  46.2 1.0 copy.13
  47.2 2.8 %copy.18 = bf16[1,1792,448]{2,1,0:T(8,128)(2,1)S(1)} copy(bf16[1,1792,448]{1,2,0:T(8,128)(2,1)} %param.11) | data formatting | bytes 3211264 | tf_op jit(solution)/shard_map/reshape;squeeze | solution.py:79
  50.0 13.3 %collective-permute-done.9 = bf16[128,1792]{0,1:T(8,128)(2,1)} collective-permute-done((bf16[128,1792]{0,1:T(8,128)(2,1)S(1)}, bf16[128,1792]{0,1:T(8,128)(2,1)}, u32[]{:S(2)}, u32[]{:S(2)}) %collective-permute-start.9) | collective-permute-done | bytes 458784 | tf_op jit(solution)/shard_map/ppermute | solution.py:27
  63.2 3.0 %add_convert_fusion.1 = bf16[128,1792]{0,1:T(8,128)(2,1)S(1)} fusion(bf16[128,1792]{0,1:T(8,128)(2,1)} %copy-done.8, bf16[128,1792]{0,1:T(8,128)(2,1)} %collective-permute-done.9, bf16[1,128,1792]{1,2,0:T(8,128)(2,1)} %copy.13, f32[1792]{0:T(1024)S(1)} %get-tuple-element.9, f32[1792]{0:T(1024)S(1)} %get-tuple-element.10, f32[1792]{0:T(1024)S(1)} %get-tuple-element.11, ...), kind=kLoop, calls=%fused_computation.109 | loop fusion | flops 3211264 | bytes 1863681 | tf_op jit(solution)/shard_map/convert_element_type | solution.py:77
  66.2 0.8 convolution_bitcast_fusion.1
  67.1 0.7 fusion.60
  67.8 0.2 copy-done.4
  68.0 0.9 copy-done.2
  68.9 0.1 fusion.50
  69.0 0.1 collective-permute-start.10
  69.1 22.5 %collective-permute-done.10 = bf16[128,1792]{0,1:T(8,128)(2,1)S(1)} collective-permute-done((bf16[128,1792]{0,1:T(8,128)(2,1)S(1)}, bf16[128,1792]{0,1:T(8,128)(2,1)S(1)}, u32[]{:S(2)}, u32[]{:S(2)}) %collective-permute-start.10) | collective-permute-done | bytes 458784 | tf_op jit(solution)/shard_map/ppermute | solution.py:27
  91.6 2.2 %fusion.36 = bf16[128,1792]{0,1:T(8,128)(2,1)} fusion(bf16[128,1792]{0,1:T(8,128)(2,1)S(1)} %collective-permute-done.10, bf16[128,1792]{0,1:T(8,128)(2,1)S(1)} %fusion.50, f32[1792]{0:T(1024)S(1)} %get-tuple-element.9, f32[1792]{0:T(1024)S(1)} %get-tuple-element.10, f32[1792]{0:T(1024)S(1)} %get-tuple-element.11, f32[1792]{0:T(1024)S(1)} %get-tuple-element.8, ...), kind=kLoop, calls=%fused_computation.89 | loop fusion | flops 2293760 | bytes 1404929 | tf_op jit(solution)/shard_map/convert_element_type | solution.py:60
  93.8 2.0 copy.10
  95.8 0.6 collective-permute-start
  96.4 9.0 %collective-permute-done.11 = bf16[128,1792]{0,1:T(8,128)(2,1)} collective-permute-done((bf16[128,1792]{0,1:T(8,128)(2,1)}, bf16[128,1792]{0,1:T(8,128)(2,1)}, u32[]{:S(2)}, u32[]{:S(2)}) %collective-permute-start.11) | collective-permute-done | bytes 458784 | tf_op jit(solution)/shard_map/ppermute | solution.py:27
  105.5 3.6 %fusion.40 = bf16[128,1792]{0,1:T(8,128)(2,1)} fusion(bf16[128,1792]{0,1:T(8,128)(2,1)} %collective-permute-done.11, bf16[128,1792]{0,1:T(8,128)(2,1)} %fusion.36, f32[1792]{0:T(1024)S(1)} %get-tuple-element.12, f32[1792]{0:T(1024)S(1)} %get-tuple-element.13, f32[1792]{0:T(1024)S(1)} %get-tuple-element.14, f32[1792]{0:T(1024)S(1)} %get-tuple-element.23, ...), kind=kLoop, calls=%fused_computation.93 | loop fusion | flops 2293760 | bytes 1404929 | tf_op jit(solution)/shard_map/convert_element_type | solution.py:60
  109.0 0.8 copy-done.6
  109.8 1.1 fusion
  110.8 2.5 %fusion.59 = f32[4,448,448]{2,1,0:T(8,128)} fusion(bf16[128,4,448]{0,2,1:T(8,128)(2,1)S(1)} %bitcast.83, f32[128,4,448]{0,2,1:T(8,128)S(1)} %copy-done.5, bf16[128,4,448]{0,2,1:T(8,128)(2,1)S(1)} %bitcast.81), kind=kOutput, calls=%fused_computation.136 | convolution fusion | flops 207814656 | bytes 5046272 | tf_op jit(solution)/shard_map/tbi,tbo->bio/dot_general | solution.py:108
  113.4 0.0 reduce-scatter.2.cloned.1.call-update
  113.4 6.3 %collective-permute-done.12 = bf16[128,1792]{0,1:T(8,128)(2,1)} collective-permute-done((bf16[128,1792]{0,1:T(8,128)(2,1)}, bf16[128,1792]{0,1:T(8,128)(2,1)}, u32[]{:S(2)}, u32[]{:S(2)}) %collective-permute-start.12) | collective-permute-done | bytes 458784 | tf_op jit(solution)/shard_map/ppermute | solution.py:27
  119.7 2.9 %fusion.44 = bf16[128,1792]{0,1:T(8,128)(2,1)S(1)} fusion(bf16[128,1792]{0,1:T(8,128)(2,1)} %collective-permute-done.12, bf16[128,1792]{0,1:T(8,128)(2,1)} %fusion.40, f32[1792]{0:T(1024)S(1)} %get-tuple-element.15, f32[1792]{0:T(1024)S(1)} %get-tuple-element.16, f32[1792]{0:T(1024)S(1)} %get-tuple-element.17, f32[1792]{0:T(1024)S(1)} %get-tuple-element.22, ...), kind=kLoop, calls=%fused_computation.97 | loop fusion | flops 2293760 | bytes 1404929 | tf_op jit(solution)/shard_map/convert_element_type | solution.py:60
  122.6 0.1 collective-permute-start.13
  122.7 1.8 collective-permute-done.13
  124.5 2.9 %fusion.48 = (bf16[128,1792]{0,1:T(8,128)(2,1)S(1)}, bf16[128,1792]{0,1:T(8,128)(2,1)S(1)}) fusion(bf16[128,1792]{0,1:T(8,128)(2,1)S(1)} %collective-permute-done.13, bf16[128,1792]{0,1:T(8,128)(2,1)S(1)} %fusion.44, f32[1792]{0:T(1024)S(1)} %get-tuple-element.18, f32[1792]{0:T(1024)S(1)} %get-tuple-element.19, f32[1792]{0:T(1024)S(1)} %get-tuple-element.20, ...), kind=kLoop, calls=%fused_computation.101 | loop fusion | flops 4587520 | bytes 2781185 | tf_op jit(solution)/shard_map/convert_element_type | solution.py:60
  127.4 0.3 collective-permute-start.2
  127.8 12.3 %collective-permute-done.2 = bf16[128,1792]{0,1:T(8,128)(2,1)S(1)} collective-permute-done((bf16[128,1792]{0,1:T(8,128)(2,1)S(1)}, bf16[128,1792]{0,1:T(8,128)(2,1)S(1)}, u32[]{:S(2)}, u32[]{:S(2)}) %collective-permute-start.2) | collective-permute-done | bytes 458784 | tf_op jit(solution)/shard_map/ppermute | solution.py:27
  140.1 1.3 fusion.8
  141.5 0.7 collective-permute-start.3
  142.1 0.3 fusion.52
  142.5 0.1 collective-permute-start.14
  142.5 1.2 collective-permute-done.14
  143.8 0.4 collective-permute-start.15
  144.1 5.8 %collective-permute-done.15 = f32[128,128]{1,0:T(8,128)S(1)} collective-permute-done((f32[128,128]{1,0:T(8,128)S(1)}, f32[128,128]{1,0:T(8,128)S(1)}, u32[]{:S(2)}, u32[]{:S(2)}) %collective-permute-start.15) | collective-permute-done | bytes 65568 | tf_op jit(solution)/shard_map/ppermute | solution.py:12
  149.9 1.5 collective-permute-start.16
  151.4 0.3 convolution_bitcast_fusion
  151.7 17.8 %collective-permute-done.16 = f32[128,128]{1,0:T(8,128)S(1)} collective-permute-done((f32[128,128]{1,0:T(8,128)S(1)}, f32[128,128]{1,0:T(8,128)S(1)}, u32[]{:S(2)}, u32[]{:S(2)}) %collective-permute-start.16) | collective-permute-done | bytes 65568 | tf_op jit(solution)/shard_map/ppermute | solution.py:12
  169.5 1.4 collective-permute-start.17
  170.9 2.2 %fusion.12 = bf16[128,1792]{0,1:T(8,128)(2,1)} fusion(bf16[128,1792]{0,1:T(8,128)(2,1)S(1)} %collective-permute-done.3, bf16[128,1792]{0,1:T(8,128)(2,1)S(1)} %fusion.8, f32[1792]{0:T(1024)S(1)} %get-tuple-element.12, f32[1792]{0:T(1024)S(1)} %get-tuple-element.13, f32[1792]{0:T(1024)S(1)} %get-tuple-element.14, f32[1792]{0:T(1024)S(1)} %get-tuple-element.23, ...), kind=kLoop, calls=%fused_computation.65 | loop fusion | flops 2293760 | bytes 1404929 | tf_op jit(solution)/shard_map/convert_element_type | solution.py:46
  173.1 1.5 collective-permute-start.4
  174.7 0.2 add_convert_fusion
  174.8 1.0 copy.17
  175.8 0.6 add_bitcast_fusion
  176.5 27.3 %collective-permute-done.4 = bf16[128,1792]{0,1:T(8,128)(2,1)} collective-permute-done((bf16[128,1792]{0,1:T(8,128)(2,1)}, bf16[128,1792]{0,1:T(8,128)(2,1)}, u32[]{:S(2)}, u32[]{:S(2)}) %collective-permute-start.4) | collective-permute-done | bytes 458784 | tf_op jit(solution)/shard_map/ppermute | solution.py:27
  203.8 2.9 %add_convert_fusion.3 = bf16[128,1792]{0,1:T(8,128)(2,1)S(1)} fusion(bf16[128,1792]{0,1:T(8,128)(2,1)} %fusion.12, bf16[128,1792]{0,1:T(8,128)(2,1)} %collective-permute-done.4, bf16[1,128,1792]{1,2,0:T(8,128)(2,1)S(1)} %copy-done.7, f32[1792]{0:T(1024)S(1)} %get-tuple-element.9, f32[1792]{0:T(1024)S(1)} %get-tuple-element.10, ...), kind=kLoop, calls=%fused_computation.111 | loop fusion | flops 3211264 | bytes 1863681 | tf_op jit(solution)/shard_map/convert_element_type | solution.py:77
  206.6 0.9 add_convert_fusion.2
  207.5 1.0 copy.16
  (27 shorter events, 0.1 us)
Async XLA Ops:
  7.2 0.8 copy-start
  7.2 201.3 %reduce-scatter.2.cloned.1.call-start = ((), (), s32[]{:S(2)}) async-start(), calls=%async_computation.1 | async-start | bytes 3899392 | tf_op jit(solution)/shard_map/reduce_scatter | solution.py:111
  9.3 2.0 collective-permute-start.6
  11.2 32.5 %copy-start.9 = (bf16[1,128,1792]{2,1,0:T(8,128)(2,1)S(1)}, bf16[1,128,1792]{2,1,0:T(8,128)(2,1)}, u32[]{:S(2)}) copy-start(bf16[1,128,1792]{2,1,0:T(8,128)(2,1)} %param.7) | copy-start | bytes 1376260
  12.6 13.8 %collective-permute-start.7 = (bf16[128,1792]{0,1:T(8,128)(2,1)S(1)}, bf16[128,1792]{0,1:T(8,128)(2,1)S(1)}, u32[]{:S(2)}, u32[]{:S(2)}) collective-permute-start(bf16[128,1792]{0,1:T(8,128)(2,1)S(1)} %fusion.20), channel_id=1, source_target_pairs={{0,2},{2,0},{1,3},{3,1},{4,6},{6,4},{5,7},{7,5},{8,10},{10,8},{9,1... | collective-permute-start | bytes 1376264 | tf_op jit(solution)/shard_map/ppermute | solution.py:27
  26.3 19.9 %copy-start.1 = (bf16[1,128,1792]{2,1,0:T(8,128)(2,1)S(1)}, bf16[1,128,1792]{2,1,0:T(8,128)(2,1)}, u32[]{:S(2)}) copy-start(bf16[1,128,1792]{2,1,0:T(8,128)(2,1)} %param.8) | copy-start | bytes 1376260
  27.7 12.1 %collective-permute-start.8 = (bf16[128,1792]{0,1:T(8,128)(2,1)S(1)}, bf16[128,1792]{0,1:T(8,128)(2,1)S(1)}, u32[]{:S(2)}, u32[]{:S(2)}) collective-permute-start(bf16[128,1792]{0,1:T(8,128)(2,1)S(1)} %fusion.24), channel_id=1, source_target_pairs={{0,4},{4,0},{1,5},{5,1},{2,6},{6,2},{3,7},{7,3},{8,12},{12,8},{9,1... | collective-permute-start | bytes 1376264 | tf_op jit(solution)/shard_map/ppermute | solution.py:27
  41.2 8.8 %copy-start.8 = (bf16[128,1792]{0,1:T(8,128)(2,1)}, bf16[128,1792]{0,1:T(8,128)(2,1)S(1)}, u32[]{:S(2)}) copy-start(bf16[128,1792]{0,1:T(8,128)(2,1)S(1)} %fusion.28) | copy-start | bytes 1376260
  41.2 22.1 %collective-permute-start.9 = (bf16[128,1792]{0,1:T(8,128)(2,1)S(1)}, bf16[128,1792]{0,1:T(8,128)(2,1)}, u32[]{:S(2)}, u32[]{:S(2)}) collective-permute-start(bf16[128,1792]{0,1:T(8,128)(2,1)S(1)} %fusion.28), channel_id=1, source_target_pairs={{0,8},{8,0},{1,9},{9,1},{2,10},{10,2},{3,11},{11,3},{4,12},{12,4},... | collective-permute-start | bytes 1376264 | tf_op jit(solution)/shard_map/ppermute | solution.py:27
  44.7 22.3 %collective-permute-start.5 = (bf16[1,128,1792]{1,2,0:T(8,128)(2,1)}, bf16[1,128,1792]{1,2,0:T(8,128)(2,1)S(1)}, u32[]{:S(2)}, u32[]{:S(2)}) collective-permute-start(bf16[1,128,1792]{1,2,0:T(8,128)(2,1)} %copy.12), channel_id=1, source_target_pairs={{16,0},{0,16},{17,1},{1,17},{18,2},{2,18},{19,3},{3,19},{20,4},{4,... | collective-permute-start | bytes 1376264 | tf_op jit(solution)/shard_map/ppermute | solution.py:33
  67.1 0.9 copy-start.4
  68.0 0.9 copy-start.2
  69.0 22.6 %collective-permute-start.10 = (bf16[128,1792]{0,1:T(8,128)(2,1)S(1)}, bf16[128,1792]{0,1:T(8,128)(2,1)S(1)}, u32[]{:S(2)}, u32[]{:S(2)}) collective-permute-start(bf16[128,1792]{0,1:T(8,128)(2,1)S(1)} %fusion.50), channel_id=1, source_target_pairs={{0,8},{8,0},{1,9},{9,1},{2,10},{10,2},{3,11},{11,3},{4,12},{12,4},... | collective-permute-start | bytes 1376264 | tf_op jit(solution)/shard_map/ppermute | solution.py:27
  93.8 11.6 %collective-permute-start.11 = (bf16[128,1792]{0,1:T(8,128)(2,1)}, bf16[128,1792]{0,1:T(8,128)(2,1)}, u32[]{:S(2)}, u32[]{:S(2)}) collective-permute-start(bf16[128,1792]{0,1:T(8,128)(2,1)} %fusion.36), channel_id=1, source_target_pairs={{0,4},{4,0},{1,5},{5,1},{2,6},{6,2},{3,7},{7,3},{8,12},{12,8},{9,1... | collective-permute-start | bytes 1376264 | tf_op jit(solution)/shard_map/ppermute | solution.py:27
  95.8 15.0 %copy-start.5 = (f32[128,4,448]{0,2,1:T(8,128)S(1)}, f32[128,4,448]{0,2,1:T(8,128)}, u32[]{:S(2)}) copy-start(f32[128,4,448]{0,2,1:T(8,128)} %copy-done.4) | copy-start | bytes 2752516
  95.8 13.2 %collective-permute-start = (bf16[1,128,1792]{1,2,0:T(8,128)(2,1)}, bf16[1,128,1792]{1,2,0:T(8,128)(2,1)S(1)}, u32[]{:S(2)}, u32[]{:S(2)}) collective-permute-start(bf16[1,128,1792]{1,2,0:T(8,128)(2,1)} %copy.10), channel_id=1, source_target_pairs={{16,0},{0,16},{17,1},{1,17},{18,2},{2,18},{19,3},{3,19},{20,4},{4,... | collective-permute-start | bytes 1376264 | tf_op jit(solution)/shard_map/ppermute | solution.py:33
  109.0 10.7 %collective-permute-start.12 = (bf16[128,1792]{0,1:T(8,128)(2,1)}, bf16[128,1792]{0,1:T(8,128)(2,1)}, u32[]{:S(2)}, u32[]{:S(2)}) collective-permute-start(bf16[128,1792]{0,1:T(8,128)(2,1)} %fusion.40), channel_id=1, source_target_pairs={{0,2},{2,0},{1,3},{3,1},{4,6},{6,4},{5,7},{7,5},{8,10},{10,8},{9,1... | collective-permute-start | bytes 1376264 | tf_op jit(solution)/shard_map/ppermute | solution.py:27
  109.0 0.8 copy-start.6
  110.8 11.9 %collective-permute-start.1 = (bf16[128,1792]{0,1:T(8,128)(2,1)}, bf16[128,1792]{0,1:T(8,128)(2,1)}, u32[]{:S(2)}, u32[]{:S(2)}) collective-permute-start(bf16[128,1792]{0,1:T(8,128)(2,1)} %fusion), channel_id=1, source_target_pairs={{0,1},{1,0},{2,3},{3,2},{4,5},{5,4},{6,7},{7,6},{8,9},{9,8},{10,11... | collective-permute-start | bytes 1376264 | tf_op jit(solution)/shard_map/ppermute | solution.py:27
  122.6 1.9 collective-permute-start.13
  127.4 12.7 %collective-permute-start.2 = (bf16[128,1792]{0,1:T(8,128)(2,1)S(1)}, bf16[128,1792]{0,1:T(8,128)(2,1)S(1)}, u32[]{:S(2)}, u32[]{:S(2)}) collective-permute-start(bf16[128,1792]{0,1:T(8,128)(2,1)S(1)} %get-tuple-element.25), channel_id=1, source_target_pairs={{0,2},{2,0},{1,3},{3,1},{4,6},{6,4},{5,7},{7,5},{8,10},{10,8},{9,1... | collective-permute-start | bytes 1376264 | tf_op jit(solution)/shard_map/ppermute | solution.py:27
  141.5 29.5 %collective-permute-start.3 = (bf16[128,1792]{0,1:T(8,128)(2,1)S(1)}, bf16[128,1792]{0,1:T(8,128)(2,1)S(1)}, u32[]{:S(2)}, u32[]{:S(2)}) collective-permute-start(bf16[128,1792]{0,1:T(8,128)(2,1)S(1)} %fusion.8), channel_id=1, source_target_pairs={{0,4},{4,0},{1,5},{5,1},{2,6},{6,2},{3,7},{7,3},{8,12},{12,8},{9,1... | collective-permute-start | bytes 1376264 | tf_op jit(solution)/shard_map/ppermute | solution.py:27
  142.4 32.2 %copy-start.3 = (f32[4,128,448]{1,2,0:T(8,128)S(1)}, f32[4,128,448]{1,2,0:T(8,128)}, u32[]{:S(2)}) copy-start(f32[4,128,448]{1,2,0:T(8,128)} %copy-done.2) | copy-start | bytes 2752516
  142.5 1.3 collective-permute-start.14
  143.8 6.1 %collective-permute-start.15 = (f32[128,128]{1,0:T(8,128)S(1)}, f32[128,128]{1,0:T(8,128)S(1)}, u32[]{:S(2)}, u32[]{:S(2)}) collective-permute-start(f32[128,128]{1,0:T(8,128)S(1)} %add.148), channel_id=1, source_target_pairs={{0,2},{1,3},{2,0},{3,1},{4,6},{5,7},{6,4},{7,5},{8,10},{9,11},{10,... | collective-permute-start | bytes 196616 | tf_op jit(solution)/shard_map/ppermute | solution.py:12
  149.9 19.5 %collective-permute-start.16 = (f32[128,128]{1,0:T(8,128)S(1)}, f32[128,128]{1,0:T(8,128)S(1)}, u32[]{:S(2)}, u32[]{:S(2)}) collective-permute-start(f32[128,128]{1,0:T(8,128)S(1)} %add.149), channel_id=1, source_target_pairs={{0,4},{1,5},{2,6},{3,7},{4,0},{5,1},{6,2},{7,3},{8,12},{9,13},{10,... | collective-permute-start | bytes 196616 | tf_op jit(solution)/shard_map/ppermute | solution.py:12
  169.5 6.3 %collective-permute-start.17 = (f32[128,128]{1,0:T(8,128)S(1)}, f32[128,128]{1,0:T(8,128)S(1)}, u32[]{:S(2)}, u32[]{:S(2)}) collective-permute-start(f32[128,128]{1,0:T(8,128)S(1)} %add.150), channel_id=1, source_target_pairs={{0,8},{1,9},{2,10},{3,11},{4,12},{5,13},{6,14},{7,15},{8,0},{9,1},... | collective-permute-start | bytes 196616 | tf_op jit(solution)/shard_map/ppermute | solution.py:12
  173.1 30.6 %collective-permute-start.4 = (bf16[128,1792]{0,1:T(8,128)(2,1)}, bf16[128,1792]{0,1:T(8,128)(2,1)}, u32[]{:S(2)}, u32[]{:S(2)}) collective-permute-start(bf16[128,1792]{0,1:T(8,128)(2,1)} %fusion.12), channel_id=1, source_target_pairs={{0,8},{8,0},{1,9},{9,1},{2,10},{10,2},{3,11},{11,3},{4,12},{12,4},... | collective-permute-start | bytes 1376264 | tf_op jit(solution)/shard_map/ppermute | solution.py:27
  174.7 29.1 %copy-start.7 = (bf16[1,128,1792]{1,2,0:T(8,128)(2,1)S(1)}, bf16[1,128,1792]{1,2,0:T(8,128)(2,1)}, u32[]{:S(2)}) copy-start(bf16[1,128,1792]{1,2,0:T(8,128)(2,1)} %copy-done.6) | copy-start | bytes 1376260
Sparse Core Ops, SparseCore 0:
  113.5 91.3 reduce-scatter.1
